TPU v7x, 32 devices: a whole 2x2x4 slice. The times are simulated.
32 devices in a mesh: seq: 4 (over z), fsdp: 8 (over y, x, core).
Axes of the slice: x: 2, y: 2, z: 4, core: 2. Of those that a mesh axis runs over, the one named last changes fastest.
Arguments:
- tokens: bfloat16 [8, 512, 768], P('fsdp', 'seq'), may hold values from -6 to 6
- positions: int32 [8, 512], P('fsdp', 'seq'), may hold values from 0 to 5117, as said below
- norm1_gain: bfloat16 [768], P('fsdp'), may hold values from 0.5 to 1.5
- qkv_weight: bfloat16 [768, 2304], P('fsdp'), may hold values from -0.57735027 to 0.57735027, as said below
- out_weight: bfloat16 [768, 768], P('fsdp'), may hold values from -6 to 6
- norm2_gain: bfloat16 [768], P('fsdp'), may hold values from 0.5 to 1.5
- in_weight: bfloat16 [768, 2304], P('fsdp'), may hold values from -0.21875 to 0.21875
- down_weight: bfloat16 [1152, 768], P(None, 'fsdp'), may hold values from -0.1875 to 0.1875
- cotangent: bfloat16 [8, 512, 768], P('fsdp', 'seq'), may hold values from -6 to 6
Outputs:
- block_out: bfloat16 [8, 512, 768], P('fsdp', 'seq')
- input_grad: bfloat16 [8, 512, 768], P('fsdp', 'seq')
- qkv_weight_grad: float32 [768, 2304], P('fsdp')
- out_weight_grad: float32 [768, 768], P('fsdp')
- in_weight_grad: float32 [768, 2304], P('fsdp')
- down_weight_grad: float32 [1152, 768], P(None, 'fsdp')
- norm1_gain_grad: float32 [768], P('fsdp')
- norm2_gain_grad: float32 [768], P('fsdp')
Inputs may be any that keep to these rules, and one draw needn't show every extreme that they name: Along each sequence the positions rise by 1 or 2 from one token to the next. `qkv_weight`: A projection matrix; every entry lies within 16 / sqrt(768) of zero.
All inputs are finite; a program needn't handle non-finite values.
Results may differ from a plain program's by a relative error of at most 0.019.
Values may be sent and summed in bfloat16 or wider, within the bound.
A program may use at most 128 MiB of HBM per device.

v0:
```python
import jax
import jax.numpy as jnp
from jax import lax
from jax.sharding import PartitionSpec as P

HEADS = 12
HEAD_DIM = 64
eps = 1e-05
theta = 160000.0


def layer_norm(values, gain_vec):
    middle = jnp.mean(values, axis=-1, keepdims=True)
    centred = values - middle
    inverse = lax.rsqrt(jnp.mean(centred * centred, axis=-1, keepdims=True) + eps)
    scaled = centred * inverse
    return (scaled * gain_vec, scaled, inverse)


def norm_back(upstream, scaled, inverse, gain_vec):
    gain_grad = jnp.sum(upstream * scaled, axis=0)
    weighted = upstream * gain_vec
    result = inverse * (
        weighted
        - jnp.mean(weighted, axis=-1, keepdims=True)
        - scaled * jnp.mean(weighted * scaled, axis=-1, keepdims=True)
    )
    return (result, gain_grad)


def rotary_tables(positions, head_size):
    half_dim = head_size // 2
    frequency = theta ** (-jnp.arange(half_dim, dtype=jnp.float32) / half_dim)
    angles = positions.astype(jnp.float32)[..., None] * frequency
    return (jnp.cos(angles)[..., None, :], jnp.sin(angles)[..., None, :])


def rotate(values, cosine_table, sine_table):
    half_dim = values.shape[-1] // 2
    first_half = values[..., :half_dim]
    second_half = values[..., half_dim:]
    return jnp.concatenate(
        [
            first_half * cosine_table - second_half * sine_table,
            second_half * cosine_table + first_half * sine_table,
        ],
        axis=-1,
    )


def rotate_back(values, cosine_table, sine_table):
    half_dim = values.shape[-1] // 2
    first_half = values[..., :half_dim]
    second_half = values[..., half_dim:]
    return jnp.concatenate(
        [
            first_half * cosine_table + second_half * sine_table,
            second_half * cosine_table - first_half * sine_table,
        ],
        axis=-1,
    )


def gelu_slope(values):
    return (
        0.5 * (1.0 + lax.erf(values * 0.7071067811865476))
        + values * jnp.exp(-0.5 * values * values) * 0.3989422804014327
    )


def local(
    tokens,
    positions,
    norm1_gain,
    qkv_weight,
    out_weight,
    norm2_gain,
    in_weight,
    down_weight,
    cotangent,
):
    f32 = jnp.float32
    low = jnp.bfloat16
    groups = lax.axis_size("seq")
    seq_dev, span_len, model_width = tokens.shape
    row_count = seq_dev * span_len
    local_heads = HEADS // groups
    group_width = local_heads * HEAD_DIM
    length = span_len * groups
    block_rows = min(512, length)
    block_count = length // block_rows
    score_scale = HEAD_DIM ** (-0.5)
    gathered = (
        lax.all_gather(qkv_weight, "fsdp", axis=0, tiled=True),
        lax.all_gather(out_weight, "fsdp", axis=0, tiled=True),
        lax.all_gather(in_weight, "fsdp", axis=0, tiled=True),
        lax.all_gather(down_weight, "fsdp", axis=1, tiled=True),
        lax.all_gather(norm1_gain, "fsdp", axis=0, tiled=True),
        lax.all_gather(norm2_gain, "fsdp", axis=0, tiled=True),
    )
    w_qkv, w_out, w_in, w_down, gain_one, gain_two = gathered
    gain_one = gain_one.astype(f32)
    gain_two = gain_two.astype(f32)
    inputs = tokens.reshape(row_count, model_width).astype(f32)
    normed_one, scaled_one, inverse_one = layer_norm(inputs, gain_one)
    normed_one = normed_one.astype(low)
    projected = jnp.dot(normed_one, w_qkv, preferred_element_type=f32).reshape(
        seq_dev, span_len, 3, HEADS, HEAD_DIM
    )
    cosine_table, sine_table = rotary_tables(positions, HEAD_DIM)
    queries = rotate(projected[:, :, 0], cosine_table, sine_table)
    key_part = rotate(projected[:, :, 1], cosine_table, sine_table)
    packed = jnp.stack([queries, key_part, projected[:, :, 2]], axis=2).astype(low)
    packed = packed.reshape(seq_dev, span_len, 3, groups, group_width)
    heads = lax.all_to_all(packed, "seq", split_axis=3, concat_axis=1, tiled=True)
    heads = heads.reshape(seq_dev, length, 3, local_heads, HEAD_DIM)
    query_rows = heads[:, :, 0]
    key_rows = heads[:, :, 1]
    value_rows = heads[:, :, 2]
    query_blocks = jnp.swapaxes(
        query_rows.reshape(seq_dev, block_count, block_rows, local_heads, HEAD_DIM), 0, 1
    )

    def attend(query_block):
        scores = (
            jnp.einsum("bqhd,bkhd->bhqk", query_block, key_rows, preferred_element_type=f32)
            * score_scale
        )
        totals = jax.nn.logsumexp(scores, axis=-1)
        probs_low = jnp.exp(scores - totals[..., None]).astype(low)
        result = jnp.einsum("bhqk,bkhd->bqhd", probs_low, value_rows, preferred_element_type=f32)
        return (result.astype(low), totals)

    attended, totals = lax.map(attend, query_blocks)
    attended = jnp.swapaxes(attended, 0, 1).reshape(seq_dev, length, local_heads, HEAD_DIM)
    outgoing = attended.reshape(seq_dev, length, 1, group_width)
    returned = lax.all_to_all(outgoing, "seq", split_axis=1, concat_axis=2, tiled=True)
    mixed_heads = returned.reshape(row_count, model_width)
    residual = inputs + jnp.dot(mixed_heads, w_out, preferred_element_type=f32)
    normed_two, scaled_two, inverse_two = layer_norm(residual, gain_two)
    normed_two = normed_two.astype(low)
    lifted = jnp.dot(normed_two, w_in, preferred_element_type=f32)
    ff_size = lifted.shape[1] // 2
    act_input = lifted[:, :ff_size]
    gate_part = lifted[:, ff_size:]
    activated = jax.nn.gelu(act_input, approximate=False)
    gated = (activated * gate_part).astype(low)
    block_out = (residual + jnp.dot(gated, w_down, preferred_element_type=f32)).astype(low)
    regathered = (
        lax.all_gather(qkv_weight, "fsdp", axis=0, tiled=True),
        lax.all_gather(out_weight, "fsdp", axis=0, tiled=True),
        lax.all_gather(in_weight, "fsdp", axis=0, tiled=True),
        lax.all_gather(down_weight, "fsdp", axis=1, tiled=True),
        lax.all_gather(norm1_gain, "fsdp", axis=0, tiled=True),
        lax.all_gather(norm2_gain, "fsdp", axis=0, tiled=True),
    )
    w_qkv, w_out, w_in, w_down, gain_low_one, gain_low_two = regathered
    gain_one = gain_low_one.astype(f32)
    gain_two = gain_low_two.astype(f32)
    upstream = cotangent.reshape(row_count, model_width)
    gated_grad = jnp.dot(upstream, w_down.T, preferred_element_type=f32)
    lifted_grad = jnp.concatenate(
        [gated_grad * gate_part * gelu_slope(act_input), gated_grad * activated], axis=1
    ).astype(low)
    normed_two_grad = jnp.dot(lifted_grad, w_in.T, preferred_element_type=f32)
    residual_part, gain_two_grad = norm_back(normed_two_grad, scaled_two, inverse_two, gain_two)
    residual_grad = upstream.astype(f32) + residual_part
    residual_low = residual_grad.astype(low)
    mixed_grad = jnp.dot(residual_low, w_out.T, preferred_element_type=f32).astype(low)
    grad_outgoing = mixed_grad.reshape(seq_dev, span_len, groups, group_width)
    grad_heads = lax.all_to_all(grad_outgoing, "seq", split_axis=2, concat_axis=1, tiled=True)
    grad_heads = grad_heads.reshape(seq_dev, length, local_heads, HEAD_DIM)
    delta_rows = jnp.sum(grad_heads.astype(f32) * attended.astype(f32), axis=-1)
    grad_blocks = jnp.swapaxes(
        grad_heads.reshape(seq_dev, block_count, block_rows, local_heads, HEAD_DIM), 0, 1
    )
    delta_blocks = jnp.swapaxes(
        jnp.swapaxes(delta_rows.reshape(seq_dev, block_count, block_rows, local_heads), 0, 1), 2, 3
    )

    def attend_back(carry, block_inputs):
        key_total, value_total = carry
        query_block, grad_block, delta_block, total_block = block_inputs
        scores = (
            jnp.einsum("bqhd,bkhd->bhqk", query_block, key_rows, preferred_element_type=f32)
            * score_scale
        )
        probs = jnp.exp(scores - total_block[..., None])
        probs_low = probs.astype(low)
        value_total = value_total + jnp.einsum(
            "bhqk,bqhd->bkhd", probs_low, grad_block, preferred_element_type=f32
        )
        prob_grad = jnp.einsum(
            "bqhd,bkhd->bhqk", grad_block, value_rows, preferred_element_type=f32
        )
        score_grad = (probs * (prob_grad - delta_block[..., None])).astype(low)
        query_grad = (
            jnp.einsum("bhqk,bkhd->bqhd", score_grad, key_rows, preferred_element_type=f32)
            * score_scale
        ).astype(low)
        key_total = key_total + jnp.einsum(
            "bhqk,bqhd->bkhd", score_grad, query_block, preferred_element_type=f32
        )
        return ((key_total, value_total), query_grad)

    zeros_state = jnp.zeros((seq_dev, length, local_heads, HEAD_DIM), f32)
    (key_total, value_total), query_grads = lax.scan(
        attend_back, (zeros_state, zeros_state), (query_blocks, grad_blocks, delta_blocks, totals)
    )
    query_grad = jnp.swapaxes(query_grads, 0, 1).reshape(seq_dev, length, group_width)
    key_grad = (key_total * score_scale).astype(low).reshape(seq_dev, length, group_width)
    value_grad = value_total.astype(low).reshape(seq_dev, length, group_width)
    grads_outgoing = jnp.stack([query_grad, key_grad, value_grad], axis=2)[:, :, :, None, :]
    grads_returned = lax.all_to_all(grads_outgoing, "seq", split_axis=1, concat_axis=3, tiled=True)
    grads_returned = grads_returned.reshape(seq_dev, span_len, 3, HEADS, HEAD_DIM).astype(f32)
    qkv_grad = jnp.stack(
        [
            rotate_back(grads_returned[:, :, 0], cosine_table, sine_table),
            rotate_back(grads_returned[:, :, 1], cosine_table, sine_table),
            grads_returned[:, :, 2],
        ],
        axis=2,
    )
    qkv_grad = qkv_grad.reshape(row_count, 3 * model_width).astype(low)
    normed_one_grad = jnp.dot(qkv_grad, w_qkv.T, preferred_element_type=f32)
    input_part, gain_one_grad = norm_back(normed_one_grad, scaled_one, inverse_one, gain_one)
    input_grad = (residual_grad + input_part).astype(low).reshape(seq_dev, span_len, model_width)
    gain_terms = (gain_one_grad, gain_two_grad)
    terms = (
        jnp.dot(normed_one.T, qkv_grad, preferred_element_type=f32),
        jnp.dot(mixed_heads.T, residual_low, preferred_element_type=f32),
        jnp.dot(normed_two.T, lifted_grad, preferred_element_type=f32),
        jnp.dot(gated.T, upstream, preferred_element_type=f32),
        gain_terms[0],
        gain_terms[1],
    )
    pieces = (
        lax.psum_scatter(terms[0], "fsdp", scatter_dimension=0, tiled=True),
        lax.psum_scatter(terms[1], "fsdp", scatter_dimension=0, tiled=True),
        lax.psum_scatter(terms[2], "fsdp", scatter_dimension=0, tiled=True),
        lax.psum_scatter(terms[3], "fsdp", scatter_dimension=1, tiled=True),
        lax.psum_scatter(terms[4], "fsdp", scatter_dimension=0, tiled=True),
        lax.psum_scatter(terms[5], "fsdp", scatter_dimension=0, tiled=True),
    )
    parts = (
        lax.psum_scatter(
            pieces[0].astype(jnp.bfloat16), "seq", scatter_dimension=0, tiled=True
        ).astype(jnp.float32),
        lax.psum_scatter(
            pieces[1].astype(jnp.bfloat16), "seq", scatter_dimension=0, tiled=True
        ).astype(jnp.float32),
        lax.psum_scatter(
            pieces[2].astype(jnp.bfloat16), "seq", scatter_dimension=0, tiled=True
        ).astype(jnp.float32),
        lax.psum_scatter(
            pieces[3].astype(jnp.bfloat16), "seq", scatter_dimension=1, tiled=True
        ).astype(jnp.float32),
        lax.psum_scatter(
            pieces[4].astype(jnp.bfloat16), "seq", scatter_dimension=0, tiled=True
        ).astype(jnp.float32),
        lax.psum_scatter(
            pieces[5].astype(jnp.bfloat16), "seq", scatter_dimension=0, tiled=True
        ).astype(jnp.float32),
    )
    summed = (
        lax.all_gather(parts[0].astype(jnp.bfloat16), "seq", axis=0, tiled=True).astype(
            jnp.float32
        ),
        lax.all_gather(parts[1].astype(jnp.bfloat16), "seq", axis=0, tiled=True).astype(
            jnp.float32
        ),
        lax.all_gather(parts[2].astype(jnp.bfloat16), "seq", axis=0, tiled=True).astype(
            jnp.float32
        ),
        lax.all_gather(parts[3].astype(jnp.bfloat16), "seq", axis=1, tiled=True).astype(
            jnp.float32
        ),
        lax.all_gather(parts[4].astype(jnp.bfloat16), "seq", axis=0, tiled=True).astype(
            jnp.float32
        ),
        lax.all_gather(parts[5].astype(jnp.bfloat16), "seq", axis=0, tiled=True).astype(
            jnp.float32
        ),
    )
    return (
        block_out.reshape(seq_dev, span_len, model_width),
        input_grad,
        summed[0],
        summed[1],
        summed[2],
        summed[3],
        summed[4],
        summed[5],
    )


def solution(mesh):
    in_specs = (
        P("fsdp", "seq", None),
        P("fsdp", "seq"),
        P("fsdp"),
        P("fsdp", None),
        P("fsdp", None),
        P("fsdp"),
        P("fsdp", None),
        P(None, "fsdp"),
        P("fsdp", "seq", None),
    )
    out_specs = (
        P("fsdp", "seq", None),
        P("fsdp", "seq", None),
        P("fsdp", None),
        P("fsdp", None),
        P("fsdp", None),
        P(None, "fsdp"),
        P("fsdp"),
        P("fsdp"),
    )
    return jax.shard_map(local, mesh=mesh, in_specs=in_specs, out_specs=out_specs, check_vma=False)
```

profile of v0, /device:TPU:0, one launch (start us, length us, event | category | flops | bytes accessed | tf_op | source)
XLA Modules:
  0.0 489.6 jit_solution(12036840399194156989)
XLA Ops:
  9.4 1.3 fusion.60
  13.1 16.1 %all-reduce.10 = (bf16[768]{0:T(1024)(128)(2,1)S(1)}, bf16[768]{0:T(1024)(128)(2,1)}) all-reduce(bf16[768]{0:T(1024)(128)(2,1)S(1)} %dynamic-update-slice, bf16[768]{0:T(1024)(128)(2,1)S(1)} %dynamic-update-slice.1), channel_id=1, replica_groups=mesh['seq'=4,'fsdp'=8] {'fsdp'}, use_global_device_ids=true, to_apply=%add | all-reduce | flops 1536 | bytes 6144
  32.8 13.7 %all-gather.5.cloned.1.call-done = bf16[768,2304]{1,0:T(8,128)(2,1)} async-done(((bf16[96,2304]{1,0:T(8,128)(2,1)}), bf16[768,2304]{1,0:T(8,128)(2,1)}) %all-gather.5.cloned.1.call-update) | async-done | bytes 3538960 | tf_op jit(solution)/shard_map/all_gather | solution.py:94
  46.6 4.5 copy.88
  51.1 2.1 convolution_bitcast_fusion
  54.4 4.6 all-to-all-start
  59.6 15.7 %all-to-all-done = bf16[1,128,3,4,192]{1,4,2,0,3:T(8,128)(2,1)S(1)} async-done(((bf16[1,128,3,4,192]{1,4,2,0,3:T(8,128)(2,1)}), bf16[1,128,3,4,192]{1,4,2,0,3:T(8,128)(2,1)S(1)}, u32[]{:S(2)}, u32[]{:S(2)}) %all-to-all-start) | async-done | bytes 589856 | tf_op jit(solution)/shard_map/all_to_all | solution.py:115
  76.8 1.7 multiply_reduce_fusion
  79.0 1.6 convolution_convert_fusion.2
  82.2 3.9 reduce.6
  86.1 2.0 reshape.502
  88.1 3.4 all-to-all-start.1
  92.4 6.4 %all-to-all-done.1 = bf16[4,2,12288]{2,1,0:T(2,128)(2,1)S(1)} async-done(((bf16[4,2,12288]{2,1,0:T(2,128)(2,1)}), bf16[4,2,12288]{2,1,0:T(2,128)(2,1)S(1)}, u32[]{:S(2)}, u32[]{:S(2)}) %all-to-all-start.1) | async-done | bytes 196640 | tf_op jit(solution)/shard_map/all_to_all | solution.py:137
  99.8 1.9 copy.95
  103.3 1.8 fusion.62
  106.5 1.7 all-gather.9.cloned.1.call-done
  108.1 3.7 fusion.58
  111.9 24.5 %all-gather.11.cloned.1.call-done = bf16[1152,768]{0,1:T(8,128)(2,1)} async-done(((bf16[1152,96]{0,1:T(8,128)(2,1)}), bf16[1152,768]{0,1:T(8,128)(2,1)}) %all-gather.11.cloned.1.call-update) | async-done | bytes 1769488 | tf_op jit(solution)/shard_map/all_gather | solution.py:97
  136.3 4.6 multiply_convert_fusion.1
  141.0 1.9 multiply_reduce_fusion.1
  143.9 1.9 fusion.49
  147.9 3.3 fusion.42
  151.3 5.2 %fusion.36 = f32[768,2304]{1,0:T(8,128)} fusion(bf16[128,1152]{1,0:T(8,128)(2,1)} %copy-done.13, bf16[128,1152]{1,0:T(8,128)(2,1)} %copy-done.14, f32[128,768]{1,0:T(8,128)S(1)} %get-tuple-element.98, f32[768]{0:T(1024)S(1)} %convert_element_type.222, f32[128]{0:T(128)} %add_rsqrt_fusion, f32[128]{0:T(128)} %copy-done.21), kind=kOutput, calls=%fused_computation.80 | convolution fusion | flops 454557696 | bytes 8065024 | tf_op jit(solution)/shard_map/dot_general | solution.py:232
  156.5 2.7 convolution_convert_fusion.1
  159.2 1.7 copy.97
  161.0 12.5 %all_to_all.54 = bf16[1,128,4,192]{1,3,0,2:T(8,128)(2,1)S(1)} all-to-all(bf16[1,128,4,192]{1,3,0,2:T(8,128)(2,1)} %bitcast.196), channel_id=1, replica_groups=mesh['seq'=4,'fsdp'=8] {'seq'}, dimensions={2} | all-to-all | bytes 393216 | tf_op jit(solution)/shard_map/all_to_all | solution.py:171
  175.0 1.7 reshape.470
  178.6 1.9 reshape.473
  181.7 1.9 multiply_convert_fusion
  186.1 28.2 %all_to_all.55 = bf16[1,512,3,1,192]{4,2,3,0,1:T(4,128)(2,1)S(1)} all-to-all(bf16[1,512,3,1,192]{4,2,3,0,1:T(4,128)(2,1)S(1)} %copy.105), channel_id=1, replica_groups=mesh['seq'=4,'fsdp'=8] {'seq'}, dimensions={1} | all-to-all | bytes 1179648 | tf_op jit(solution)/shard_map/all_to_all | solution.py:214
  216.3 4.2 fusion.46
  220.6 1.8 convert_element_type.251
  222.5 17.1 %reduce-scatter.23.cloned.1.call-done = f32[1152,96]{0,1:T(8,128)} async-done(((f32[1152,768]{0,1:T(8,128)}), f32[1152,96]{0,1:T(8,128)}) %reduce-scatter.23.cloned.1.call-update) | async-done | bytes 442384 | tf_op jit(solution)/shard_map/reduce_scatter | solution.py:241
  239.6 1.7 convert_element_type.255
  241.4 67.3 %reduce-scatter.19.cloned.1.call-done = f32[96,2304]{1,0:T(8,128)} async-done(((f32[768,2304]{1,0:T(8,128)}), f32[96,2304]{1,0:T(8,128)}) %reduce-scatter.19.cloned.1.call-update) | async-done | bytes 884752 | tf_op jit(solution)/shard_map/reduce_scatter | solution.py:240
  308.7 2.0 convert_element_type.253
  312.6 1.3 fusion.4
  313.9 3.4 fusion.31
  317.4 60.3 %reduce-scatter.11.cloned.1.call-done = f32[96,2304]{1,0:T(8,128)} async-done(((f32[768,2304]{1,0:T(8,128)}), f32[96,2304]{1,0:T(8,128)}) %reduce-scatter.11.cloned.1.call-update) | async-done | bytes 884752 | tf_op jit(solution)/shard_map/reduce_scatter | solution.py:238
  377.7 2.0 convert_element_type.249
  379.7 12.8 %all-reduce.9 = (bf16[768]{0:T(1024)(128)(2,1)S(1)}, bf16[768]{0:T(1024)(128)(2,1)S(1)}) all-reduce(f32[768]{0:T(1024)S(1)} %get-tuple-element.48, f32[768]{0:T(1024)S(1)} %copy-done.26), channel_id=10, replica_groups=mesh['seq'=4,'fsdp'=8] {'fsdp'}, use_global_device_ids=true, to_apply=%region_20.21.clone | all-reduce | flops 1536 | bytes 9216
  392.6 11.7 %all-reduce.12 = (bf16[96]{0:T(256)(128)(2,1)S(1)}, bf16[96]{0:T(256)(128)(2,1)S(1)}) all-reduce(bf16[96]{0:T(256)(128)(2,1)S(1)} %dynamic-slice.19, bf16[96]{0:T(256)(128)(2,1)S(1)} %dynamic-slice.18), channel_id=11, replica_groups=mesh['seq'=4,'fsdp'=8] {'seq'}, use_global_device_ids=true, to_apply=%region_21.22.clone | all-reduce | flops 192 | bytes 768
  404.9 8.3 %all-reduce.11 = (bf16[96]{0:T(256)(128)(2,1)S(1)}, bf16[96]{0:T(256)(128)(2,1)S(1)}) all-reduce(bf16[96]{0:T(256)(128)(2,1)S(1)} %dynamic-update-slice.2, bf16[96]{0:T(256)(128)(2,1)S(1)} %dynamic-update-slice.3), channel_id=1, replica_groups=mesh['seq'=4,'fsdp'=8] {'seq'}, use_global_device_ids=true, to_apply=%add.2 | all-reduce | flops 192 | bytes 768
  415.1 13.9 %all_gather.49 = bf16[96,768]{1,0:T(8,128)(2,1)S(1)} all-gather(bf16[24,768]{1,0:T(8,128)(2,1)} %reduce-scatter.17.cloned.1.call-done), channel_id=1, replica_groups=mesh['seq'=4,'fsdp'=8] {'seq'}, dimensions={0}, use_global_device_ids=true | all-gather | bytes 184320 | tf_op jit(solution)/shard_map/all_gather | solution.py:269
  429.7 14.9 %all_gather.51 = bf16[1152,96]{0,1:T(8,128)(2,1)S(1)} all-gather(bf16[1152,24]{0,1:T(8,128)(2,1)} %reduce-scatter.25.cloned.1.call-done), channel_id=1, replica_groups=mesh['seq'=4,'fsdp'=8] {'seq'}, dimensions={1}, use_global_device_ids=true | all-gather | bytes 276480 | tf_op jit(solution)/shard_map/all_gather | solution.py:275
  445.4 17.3 %all_gather.50 = bf16[96,2304]{1,0:T(8,128)(2,1)S(1)} all-gather(bf16[24,2304]{1,0:T(8,128)(2,1)} %reduce-scatter.21.cloned.1.call-done), channel_id=1, replica_groups=mesh['seq'=4,'fsdp'=8] {'seq'}, dimensions={0}, use_global_device_ids=true | all-gather | bytes 552960 | tf_op jit(solution)/shard_map/all_gather | solution.py:272
  463.7 2.5 reduce-scatter.13.cloned.1.call-done
  466.2 15.6 %all_gather.48 = bf16[96,2304]{1,0:T(8,128)(2,1)S(1)} all-gather(bf16[24,2304]{1,0:T(8,128)(2,1)} %reduce-scatter.13.cloned.1.call-done), channel_id=1, replica_groups=mesh['seq'=4,'fsdp'=8] {'seq'}, dimensions={0}, use_global_device_ids=true | all-gather | bytes 552960 | tf_op jit(solution)/shard_map/all_gather | solution.py:266
  (154 shorter events, 36.3 us)
Async XLA Ops:
  7.2 39.4 %all-gather.5.cloned.1.call-start = ((), (), s32[]{:S(2)}) async-start(), calls=%async_computation.12 | async-start | bytes 3981312 | tf_op jit(solution)/shard_map/all_gather | solution.py:94
  7.9 95.4 %all-gather.7.cloned.1.call-start = ((), (), s32[]{:S(2)}) async-start(), calls=%async_computation.13 | async-start | bytes 1327104 | tf_op jit(solution)/shard_map/all_gather | solution.py:95
  8.6 99.5 %all-gather.9.cloned.1.call-start = ((), (), s32[]{:S(2)}) async-start(), calls=%async_computation.14 | async-start | bytes 3981312 | tf_op jit(solution)/shard_map/all_gather | solution.py:96
  30.2 20.8 %copy-start.19 = (f32[128]{0:T(128)}, f32[128]{0:T(128)S(1)}, u32[]{:S(2)}) copy-start(f32[128]{0:T(128)S(1)} %broadcast_multiply_fusion.5) | copy-start | bytes 1540
  31.4 19.7 %copy-start.23 = (f32[128]{0:T(128)}, f32[128]{0:T(128)S(1)}, u32[]{:S(2)}) copy-start(f32[128]{0:T(128)S(1)} %add_rsqrt_fusion.1) | copy-start | bytes 1540
  51.1 2.3 copy-start.15
  51.1 2.3 copy-start.17
  54.4 20.9 %all-to-all-start = ((bf16[1,128,3,4,192]{1,4,2,0,3:T(8,128)(2,1)}), bf16[1,128,3,4,192]{1,4,2,0,3:T(8,128)(2,1)S(1)}, u32[]{:S(2)}, u32[]{:S(2)}) async-start(bf16[1,128,3,4,192]{1,4,2,0,3:T(8,128)(2,1)} %pad_maximum_fusion), calls=%async_computation | async-start | bytes 1179648 | tf_op jit(solution)/shard_map/all_to_all | solution.py:115
  59.0 77.3 %all-gather.11.cloned.1.call-start = ((), (), s32[]{:S(2)}) async-start(), calls=%async_computation.15 | async-start | bytes 1990656 | tf_op jit(solution)/shard_map/all_gather | solution.py:97
  80.6 22.7 %copy-start.9 = (bf16[3,64,512]{2,1,0:T(8,128)(2,1)}, bf16[3,64,512]{2,1,0:T(8,128)(2,1)S(1)}, u32[]{:S(2)}) copy-start(bf16[3,64,512]{2,1,0:T(8,128)(2,1)S(1)} %convolution_convert_fusion.2) | copy-start | bytes 589828
  88.1 10.6 %all-to-all-start.1 = ((bf16[4,2,12288]{2,1,0:T(2,128)(2,1)}), bf16[4,2,12288]{2,1,0:T(2,128)(2,1)S(1)}, u32[]{:S(2)}, u32[]{:S(2)}) async-start(bf16[4,2,12288]{2,1,0:T(2,128)(2,1)} %reshape.502), calls=%async_computation.1 | async-start | bytes 393216 | tf_op jit(solution)/shard_map/all_to_all | solution.py:137
  91.5 129.1 %reduce-scatter.15.cloned.1.call-start = ((), (), s32[]{:S(2)}) async-start(), calls=%async_computation.18 | async-start | bytes 2654208 | tf_op jit(solution)/shard_map/reduce_scatter | solution.py:239
  105.2 0.6 copy-start.21
  136.3 4.6 copy-start.4
  136.3 4.6 copy-start.22
  136.3 4.6 copy-start.25
  140.9 2.2 copy-start.13
  140.9 2.2 copy-start.14
  140.9 2.0 copy-start.12
  141.0 2.9 copy-start.8
  143.1 0.7 copy-start.1
  145.8 93.8 %reduce-scatter.23.cloned.1.call-start = ((), (), s32[]{:S(2)}) async-start(), calls=%async_computation.22 | async-start | bytes 3981312 | tf_op jit(solution)/shard_map/reduce_scatter | solution.py:241
  147.2 0.7 copy-start.5
  151.2 157.4 %reduce-scatter.19.cloned.1.call-start = ((), (), s32[]{:S(2)}) async-start(), calls=%async_computation.20 | async-start | bytes 7962624 | tf_op jit(solution)/shard_map/reduce_scatter | solution.py:240
  156.5 221.2 %reduce-scatter.11.cloned.1.call-start = ((), (), s32[]{:S(2)}) async-start(), calls=%async_computation.16 | async-start | bytes 7962624 | tf_op jit(solution)/shard_map/reduce_scatter | solution.py:238
  173.5 0.7 copy-start.10
  180.5 3.1 copy-start.3
  183.7 1.0 copy-start.7
  215.2 0.7 copy-start.16
  215.3 0.7 copy-start.18
  215.4 0.9 copy-start
  215.4 0.9 copy-start.20
  215.4 0.9 copy-start.24
  220.5 92.1 %copy-start.6 = (bf16[128,1152]{1,0:T(8,128)(2,1)S(1)}, bf16[128,1152]{1,0:T(8,128)(2,1)}, u32[]{:S(2)}) copy-start(bf16[128,1152]{1,0:T(8,128)(2,1)} %copy-done.5) | copy-start | bytes 884740
  220.5 92.1 %copy-start.11 = (bf16[1152,768]{0,1:T(8,128)(2,1)S(1)}, bf16[1152,768]{0,1:T(8,128)(2,1)}, u32[]{:S(2)}) copy-start(bf16[1152,768]{0,1:T(8,128)(2,1)} %all-gather.11.cloned.1.call-done) | copy-start | bytes 5308420
  220.5 194.6 %reduce-scatter.17.cloned.1.call-start = ((), (), s32[]{:S(2)}) async-start(), calls=%async_computation.19 | async-start | bytes 184320 | tf_op jit(solution)/shard_map/reduce_scatter | solution.py:249
  222.4 207.3 %reduce-scatter.25.cloned.1.call-start = ((), (), s32[]{:S(2)}) async-start(), calls=%async_computation.23 | async-start | bytes 276480
  241.3 204.1 %reduce-scatter.21.cloned.1.call-start = ((), (), s32[]{:S(2)}) async-start(), calls=%async_computation.21 | async-start | bytes 552960 | tf_op jit(solution)/shard_map/reduce_scatter | solution.py:252
  310.7 155.6 %reduce-scatter.13.cloned.1.call-start = ((), (), s32[]{:S(2)}) async-start(), calls=%async_computation.17 | async-start | bytes 552960 | tf_op jit(solution)/shard_map/reduce_scatter | solution.py:246
  313.9 65.8 %copy-start.26 = (f32[768]{0:T(1024)S(1)}, f32[768]{0:T(1024)}, u32[]{:S(2)}) copy-start(f32[768]{0:T(1024)} %get-tuple-element.46) | copy-start | bytes 9220
  313.9 100.3 %copy-start.2 = (f32[128,768]{1,0:T(8,128)S(1)}, f32[128,768]{1,0:T(8,128)}, u32[]{:S(2)}) copy-start(f32[128,768]{1,0:T(8,128)} %copy-done.1) | copy-start | bytes 1179652
Sparse Core Ops, SparseCore 0:
  9.9 36.6 all-gather.4
  48.4 23.9 all-gather.6
  74.3 33.8 all-gather.8
  109.9 26.3 all-gather.10
  145.9 42.3 reduce-scatter.14
  191.6 47.9 reduce-scatter.22
  243.1 65.4 reduce-scatter.18
  312.2 65.4 reduce-scatter.10
  379.9 19.4 reduce-scatter.16
  401.6 17.8 reduce-scatter.24
  422.4 21.0 reduce-scatter.20
  446.2 19.9 reduce-scatter.12
where the time goes:
time: 491 us; the launch traced here: 490 us
  waiting for transfers between devices  212 us (43%)
  blocking collectives  151 us (31%)
  matrix products  43 us (9%)
  local copies, waits for them, and re-layouts  30.4 us (6%)
  other arithmetic  27.2 us (6%)
  between operations  17.3 us (4%)
  starting transfers between devices  8.59 us (2%)
    reduce_scatter x1, waiting for transfers between devices, local(): lax.psum_scatter(terms[2], 'fsdp', scatter_dimension=0, tiled=True)  67.3 us
    reduce_scatter x1, waiting for transfers between devices, local(): lax.psum_scatter(terms[0], 'fsdp', scatter_dimension=0, tiled=True)  60.3 us
    unnamed x4, blocking collectives  48.9 us
    all_to_all x1, blocking collectives, local(): lax.all_to_all(grads_outgoing, 'seq', split_axis=1, concat_axis=3, tiled=...  28.2 us
    all_gather x1, waiting for transfers between devices, local(): lax.all_gather(down_weight, 'fsdp', axis=1, tiled=True)  24.5 us
    all_gather x1, blocking collectives, local(): lax.all_gather(parts[2].astype(jnp.bfloat16), 'seq', axis=0, tiled=True)  17.3 us
    reduce_scatter x1, waiting for transfers between devices, local(): lax.psum_scatter(terms[3], 'fsdp', scatter_dimension=1, tiled=True)  17.1 us
    all_to_all x1, waiting for transfers between devices, local(): lax.all_to_all(packed, 'seq', split_axis=3, concat_axis=1, tiled=True)  15.7 us
  transfers between devices with their start and end apart: 14, of which 9 were waited for; matrix products, arithmetic and copies ran while one was open for 18% of the time, Pallas kernels for 0%

commit v1 on v0

--- a/solution.py
+++ b/solution.py
@@ -7,6 +7,29 @@
 HEAD_DIM = 64
 eps = 1e-05
 theta = 160000.0
+
+
+def in_blocks(array, dim, devices):
+    before, after = (array.shape[:dim], array.shape[dim + 1 :])
+    return jnp.moveaxis(array.reshape(*before, devices, -1, *after), dim, 0)
+
+
+def joined_along(tiles, dim):
+    tiles = jnp.moveaxis(tiles, 0, dim)
+    dims = tiles.shape
+    return tiles.reshape(*dims[:dim], dims[dim] * dims[dim + 1], *dims[dim + 2 :])
+
+
+def sent_to_each(shard, axis, split_dim, concat_dim):
+    count, index = (lax.axis_size(axis), lax.axis_index(axis))
+    blocks = in_blocks(shard, split_dim, count)
+    out = blocks
+    for step in range(1, count):
+        target, source = ((index + step) % count, (index - step) % count)
+        sent = lax.dynamic_index_in_dim(blocks, target, 0)
+        partner_block = lax.ppermute(sent, axis, [(i, (i + step) % count) for i in range(count)])
+        out = lax.dynamic_update_slice_in_dim(out, partner_block, source, axis=0)
+    return joined_along(out, concat_dim)
 
 
 def layer_norm(values, gain_vec):
@@ -211,7 +234,7 @@
     key_grad = (key_total * score_scale).astype(low).reshape(seq_dev, length, group_width)
     value_grad = value_total.astype(low).reshape(seq_dev, length, group_width)
     grads_outgoing = jnp.stack([query_grad, key_grad, value_grad], axis=2)[:, :, :, None, :]
-    grads_returned = lax.all_to_all(grads_outgoing, "seq", split_axis=1, concat_axis=3, tiled=True)
+    grads_returned = sent_to_each(grads_outgoing, "seq", 1, 3)
     grads_returned = grads_returned.reshape(seq_dev, span_len, 3, HEADS, HEAD_DIM).astype(f32)
     qkv_grad = jnp.stack(
         [

time: 491 us -> 491 us (level)
  blocking collectives: 151 us -> 111 us
  waiting for transfers between devices: 212 us -> 236 us
  local copies, waits for them, and re-layouts: 30.4 us -> 36.3 us
  starting transfers between devices: 8.59 us -> 14.1 us
  matrix products: 43 us -> 48.5 us
    all_to_all x2 -> x0, blocking collectives: 40.7 us -> none  [the longest x1 28.2 us: local(): lax.all_to_all(grads_outgoing, 'seq', split_axis=1, concat_axis=3, tiled=...]
    ppermute x0 -> x3, waiting for transfers between devices: none -> 13.9 us  [sent_to_each(): lax.ppermute(sent, axis, [(i, (i + step) % count) for i in range(count)])]
    all_to_all x0 -> x1, waiting for transfers between devices: none -> 8.02 us  [local(): lax.all_to_all(grad_outgoing, 'seq', split_axis=2, concat_axis=1, tiled=T...]
    unnamed x70 -> x68, local copies, waits for them, and re-layouts: 10.6 us -> 13 us
  transfers between devices with their start and end apart: 14 -> 18, of which waited for: 9 -> 12; matrix products, arithmetic and copies ran while one was open for 18% -> 20% of each run, Pallas kernels for 0% -> 0%
where the time goes in v1:
time: 491 us; the launch traced here: 490 us
  waiting for transfers between devices  236 us (48%)
  blocking collectives  111 us (23%)
  matrix products  48.5 us (10%)
  local copies, waits for them, and re-layouts  36.3 us (7%)
  other arithmetic  27.2 us (6%)
  between operations  17.4 us (4%)
  starting transfers between devices  14.1 us (3%)
    reduce_scatter x1, waiting for transfers between devices, local(): lax.psum_scatter(terms[2], 'fsdp', scatter_dimension=0, tiled=True)  67.2 us
    reduce_scatter x1, waiting for transfers between devices, local(): lax.psum_scatter(terms[0], 'fsdp', scatter_dimension=0, tiled=True)  60.3 us
    unnamed x4, blocking collectives  48.9 us
    all_gather x1, waiting for transfers between devices, local(): lax.all_gather(down_weight, 'fsdp', axis=1, tiled=True)  24.4 us
    reduce_scatter x1, waiting for transfers between devices, local(): lax.psum_scatter(terms[3], 'fsdp', scatter_dimension=1, tiled=True)  19 us
    all_gather x1, blocking collectives, local(): lax.all_gather(parts[2].astype(jnp.bfloat16), 'seq', axis=0, tiled=True)  17.3 us
    all_to_all x1, waiting for transfers between devices, local(): lax.all_to_all(packed, 'seq', split_axis=3, concat_axis=1, tiled=True)  15.7 us
    all_gather x1, blocking collectives, local(): lax.all_gather(parts[0].astype(jnp.bfloat16), 'seq', axis=0, tiled=True)  15.6 us
  transfers between devices with their start and end apart: 18, of which 12 were waited for; matrix products, arithmetic and copies ran while one was open for 20% of the time, Pallas kernels for 0%

profile of v1, /device:TPU:0, one launch (start us, length us, event | category | flops | bytes accessed | tf_op | source)
XLA Modules:
  0.0 489.8 jit_solution(17406953737559331755)
XLA Ops:
  13.1 16.1 %all-reduce.10 = (bf16[768]{0:T(1024)(128)(2,1)S(1)}, bf16[768]{0:T(1024)(128)(2,1)}) all-reduce(bf16[768]{0:T(1024)(128)(2,1)S(1)} %dynamic-update-slice, bf16[768]{0:T(1024)(128)(2,1)S(1)} %dynamic-update-slice.1), channel_id=1, replica_groups=mesh['seq'=4,'fsdp'=8] {'fsdp'}, use_global_device_ids=true, to_apply=%add | all-reduce | flops 1536 | bytes 6144
  32.8 13.7 %all-gather.5.cloned.1.call-done = bf16[768,2304]{1,0:T(8,128)(2,1)} async-done(((bf16[96,2304]{1,0:T(8,128)(2,1)}), bf16[768,2304]{1,0:T(8,128)(2,1)}) %all-gather.5.cloned.1.call-update) | async-done | bytes 3538960 | tf_op jit(solution)/shard_map/all_gather | solution.py:117
  46.6 4.5 copy.55
  51.1 2.1 convolution_bitcast_fusion
  54.4 4.6 all-to-all-start
  59.6 15.7 %all-to-all-done = bf16[1,128,3,4,192]{1,4,2,0,3:T(8,128)(2,1)S(1)} async-done(((bf16[1,128,3,4,192]{1,4,2,0,3:T(8,128)(2,1)}), bf16[1,128,3,4,192]{1,4,2,0,3:T(8,128)(2,1)S(1)}, u32[]{:S(2)}, u32[]{:S(2)}) %all-to-all-start) | async-done | bytes 589856 | tf_op jit(solution)/shard_map/all_to_all | solution.py:138
  82.2 3.9 reduce.6
  86.1 2.0 reshape.503
  88.1 3.4 all-to-all-start.1
  92.4 6.4 %all-to-all-done.1 = bf16[4,2,12288]{2,1,0:T(2,128)(2,1)S(1)} async-done(((bf16[4,2,12288]{2,1,0:T(2,128)(2,1)}), bf16[4,2,12288]{2,1,0:T(2,128)(2,1)S(1)}, u32[]{:S(2)}, u32[]{:S(2)}) %all-to-all-start.1) | async-done | bytes 196640 | tf_op jit(solution)/shard_map/all_to_all | solution.py:160
  99.8 1.9 copy.62
  103.3 1.8 fusion.65
  106.4 1.8 all-gather.9.cloned.1.call-done
  108.2 3.7 fusion.61
  111.9 24.4 %all-gather.11.cloned.1.call-done = bf16[1152,768]{0,1:T(8,128)(2,1)} async-done(((bf16[1152,96]{0,1:T(8,128)(2,1)}), bf16[1152,768]{0,1:T(8,128)(2,1)}) %all-gather.11.cloned.1.call-update) | async-done | bytes 1769488 | tf_op jit(solution)/shard_map/all_gather | solution.py:120
  136.3 4.6 multiply_convert_fusion.1
  141.0 1.9 multiply_reduce_fusion.1
  143.9 1.9 fusion.52
  147.9 3.3 fusion.45
  151.3 5.2 %fusion.39 = f32[768,2304]{1,0:T(8,128)} fusion(bf16[128,1152]{1,0:T(8,128)(2,1)} %copy-done.11, bf16[128,1152]{1,0:T(8,128)(2,1)} %copy-done.12, f32[128,768]{1,0:T(8,128)S(1)} %get-tuple-element.101, f32[768]{0:T(1024)S(1)} %convert_element_type.219, f32[128]{0:T(128)} %add_rsqrt_fusion, f32[128]{0:T(128)} %copy-done.19), kind=kOutput, calls=%fused_computation.82 | convolution fusion | flops 454557696 | bytes 8065024 | tf_op jit(solution)/shard_map/dot_general | solution.py:255
  156.5 2.7 convolution_convert_fusion.1
  159.2 1.7 copy.64
  161.0 4.6 all-to-all-start.2
  165.6 8.0 %all-to-all-done.2 = bf16[1,128,4,192]{1,3,0,2:T(8,128)(2,1)} async-done(((bf16[1,128,4,192]{1,3,0,2:T(8,128)(2,1)}), bf16[1,128,4,192]{1,3,0,2:T(8,128)(2,1)}, u32[]{:S(2)}, u32[]{:S(2)}) %all-to-all-start.2) | async-done | bytes 196640 | tf_op jit(solution)/shard_map/all_to_all | solution.py:194
  173.6 1.8 copy.66
  179.0 1.9 reshape.475
  182.0 1.9 multiply_convert_fusion
  185.2 2.0 fusion.7
  188.8 2.8 fusion.6
  193.3 2.3 fusion.5
  199.1 7.3 %collective-permute-done = bf16[1,1,128,3,1,192]{2,5,0,3,4,1:T(8,128)(2,1)S(1)} collective-permute-done((bf16[1,1,128,3,1,192]{2,5,0,3,4,1:T(8,128)(2,1)S(1)}, bf16[1,1,128,3,1,192]{2,5,0,3,4,1:T(8,128)(2,1)S(1)}, u32[]{:S(2)}, u32[]{:S(2)}) %collective-permute-start) | collective-permute-done | bytes 147488 | tf_op jit(solution)/shard_map/ppermute | solution.py:30
  206.9 6.7 %collective-permute-done.1 = bf16[1,1,128,3,1,192]{2,5,0,3,4,1:T(8,128)(2,1)S(1)} collective-permute-done((bf16[1,1,128,3,1,192]{2,5,0,3,4,1:T(8,128)(2,1)S(1)}, bf16[1,1,128,3,1,192]{2,5,0,3,4,1:T(8,128)(2,1)S(1)}, u32[]{:S(2)}, u32[]{:S(2)}) %collective-permute-start.1) | collective-permute-done | bytes 147488 | tf_op jit(solution)/shard_map/ppermute | solution.py:30
  214.6 4.1 fusion.49
  218.8 1.8 convert_element_type.247
  220.7 19.0 %reduce-scatter.23.cloned.1.call-done = f32[1152,96]{0,1:T(8,128)} async-done(((f32[1152,768]{0,1:T(8,128)}), f32[1152,96]{0,1:T(8,128)}) %reduce-scatter.23.cloned.1.call-update) | async-done | bytes 442384 | tf_op jit(solution)/shard_map/reduce_scatter | solution.py:264
  241.4 67.2 %reduce-scatter.19.cloned.1.call-done = f32[96,2304]{1,0:T(8,128)} async-done(((f32[768,2304]{1,0:T(8,128)}), f32[96,2304]{1,0:T(8,128)}) %reduce-scatter.19.cloned.1.call-update) | async-done | bytes 884752 | tf_op jit(solution)/shard_map/reduce_scatter | solution.py:263
  308.7 2.0 convert_element_type.249
  314.0 3.5 fusion.34
  317.4 60.3 %reduce-scatter.11.cloned.1.call-done = f32[96,2304]{1,0:T(8,128)} async-done(((f32[768,2304]{1,0:T(8,128)}), f32[96,2304]{1,0:T(8,128)}) %reduce-scatter.11.cloned.1.call-update) | async-done | bytes 884752 | tf_op jit(solution)/shard_map/reduce_scatter | solution.py:261
  377.7 2.0 convert_element_type.245
  379.8 12.8 %all-reduce.9 = (bf16[768]{0:T(1024)(128)(2,1)S(1)}, bf16[768]{0:T(1024)(128)(2,1)S(1)}) all-reduce(f32[768]{0:T(1024)S(1)} %get-tuple-element.48, f32[768]{0:T(1024)S(1)} %copy-done.24), channel_id=10, replica_groups=mesh['seq'=4,'fsdp'=8] {'fsdp'}, use_global_device_ids=true, to_apply=%region_20.21.clone | all-reduce | flops 1536 | bytes 9216
  392.7 11.7 %all-reduce.12 = (bf16[96]{0:T(256)(128)(2,1)S(1)}, bf16[96]{0:T(256)(128)(2,1)S(1)}) all-reduce(bf16[96]{0:T(256)(128)(2,1)S(1)} %dynamic-slice.19, bf16[96]{0:T(256)(128)(2,1)S(1)} %dynamic-slice.18), channel_id=11, replica_groups=mesh['seq'=4,'fsdp'=8] {'seq'}, use_global_device_ids=true, to_apply=%region_21.22.clone | all-reduce | flops 192 | bytes 768
  404.9 8.3 %all-reduce.11 = (bf16[96]{0:T(256)(128)(2,1)S(1)}, bf16[96]{0:T(256)(128)(2,1)S(1)}) all-reduce(bf16[96]{0:T(256)(128)(2,1)S(1)} %dynamic-update-slice.2, bf16[96]{0:T(256)(128)(2,1)S(1)} %dynamic-update-slice.3), channel_id=1, replica_groups=mesh['seq'=4,'fsdp'=8] {'seq'}, use_global_device_ids=true, to_apply=%add.2 | all-reduce | flops 192 | bytes 768
  415.2 13.9 %all_gather.49 = bf16[96,768]{1,0:T(8,128)(2,1)S(1)} all-gather(bf16[24,768]{1,0:T(8,128)(2,1)} %reduce-scatter.17.cloned.1.call-done), channel_id=1, replica_groups=mesh['seq'=4,'fsdp'=8] {'seq'}, dimensions={0}, use_global_device_ids=true | all-gather | bytes 184320 | tf_op jit(solution)/shard_map/all_gather | solution.py:292
  429.8 14.9 %all_gather.51 = bf16[1152,96]{0,1:T(8,128)(2,1)S(1)} all-gather(bf16[1152,24]{0,1:T(8,128)(2,1)} %reduce-scatter.25.cloned.1.call-done), channel_id=1, replica_groups=mesh['seq'=4,'fsdp'=8] {'seq'}, dimensions={1}, use_global_device_ids=true | all-gather | bytes 276480 | tf_op jit(solution)/shard_map/all_gather | solution.py:298
  445.5 17.3 %all_gather.50 = bf16[96,2304]{1,0:T(8,128)(2,1)S(1)} all-gather(bf16[24,2304]{1,0:T(8,128)(2,1)} %reduce-scatter.21.cloned.1.call-done), channel_id=1, replica_groups=mesh['seq'=4,'fsdp'=8] {'seq'}, dimensions={0}, use_global_device_ids=true | all-gather | bytes 552960 | tf_op jit(solution)/shard_map/all_gather | solution.py:295
  463.8 2.6 reduce-scatter.13.cloned.1.call-done
  466.4 15.6 %all_gather.48 = bf16[96,2304]{1,0:T(8,128)(2,1)S(1)} all-gather(bf16[24,2304]{1,0:T(8,128)(2,1)} %reduce-scatter.13.cloned.1.call-done), channel_id=1, replica_groups=mesh['seq'=4,'fsdp'=8] {'seq'}, dimensions={0}, use_global_device_ids=true | all-gather | bytes 552960 | tf_op jit(solution)/shard_map/all_gather | solution.py:289
  (162 shorter events, 49.0 us)
Async XLA Ops:
  7.2 39.4 %all-gather.5.cloned.1.call-start = ((), (), s32[]{:S(2)}) async-start(), calls=%async_computation.11 | async-start | bytes 3981312 | tf_op jit(solution)/shard_map/all_gather | solution.py:117
  7.9 95.4 %all-gather.7.cloned.1.call-start = ((), (), s32[]{:S(2)}) async-start(), calls=%async_computation.12 | async-start | bytes 1327104 | tf_op jit(solution)/shard_map/all_gather | solution.py:118
  8.6 99.5 %all-gather.9.cloned.1.call-start = ((), (), s32[]{:S(2)}) async-start(), calls=%async_computation.13 | async-start | bytes 3981312 | tf_op jit(solution)/shard_map/all_gather | solution.py:119
  30.2 20.8 %copy-start.17 = (f32[128]{0:T(128)}, f32[128]{0:T(128)S(1)}, u32[]{:S(2)}) copy-start(f32[128]{0:T(128)S(1)} %broadcast_multiply_fusion.5) | copy-start | bytes 1540
  31.4 19.7 %copy-start.21 = (f32[128]{0:T(128)}, f32[128]{0:T(128)S(1)}, u32[]{:S(2)}) copy-start(f32[128]{0:T(128)S(1)} %add_rsqrt_fusion.1) | copy-start | bytes 1540
  51.1 2.2 copy-start.13
  51.1 2.2 copy-start.15
  54.4 20.9 %all-to-all-start = ((bf16[1,128,3,4,192]{1,4,2,0,3:T(8,128)(2,1)}), bf16[1,128,3,4,192]{1,4,2,0,3:T(8,128)(2,1)S(1)}, u32[]{:S(2)}, u32[]{:S(2)}) async-start(bf16[1,128,3,4,192]{1,4,2,0,3:T(8,128)(2,1)} %pad_maximum_fusion), calls=%async_computation | async-start | bytes 1179648 | tf_op jit(solution)/shard_map/all_to_all | solution.py:138
  59.0 77.3 %all-gather.11.cloned.1.call-start = ((), (), s32[]{:S(2)}) async-start(), calls=%async_computation.14 | async-start | bytes 1990656 | tf_op jit(solution)/shard_map/all_gather | solution.py:120
  80.6 22.7 %copy-start.8 = (bf16[3,64,512]{2,1,0:T(8,128)(2,1)}, bf16[3,64,512]{2,1,0:T(8,128)(2,1)S(1)}, u32[]{:S(2)}) copy-start(bf16[3,64,512]{2,1,0:T(8,128)(2,1)S(1)} %convolution_convert_fusion.2) | copy-start | bytes 589828
  88.1 10.6 %all-to-all-start.1 = ((bf16[4,2,12288]{2,1,0:T(2,128)(2,1)}), bf16[4,2,12288]{2,1,0:T(2,128)(2,1)S(1)}, u32[]{:S(2)}, u32[]{:S(2)}) async-start(bf16[4,2,12288]{2,1,0:T(2,128)(2,1)} %reshape.503), calls=%async_computation.1 | async-start | bytes 393216 | tf_op jit(solution)/shard_map/all_to_all | solution.py:160
  91.4 127.4 %reduce-scatter.15.cloned.1.call-start = ((), (), s32[]{:S(2)}) async-start(), calls=%async_computation.17 | async-start | bytes 2654208 | tf_op jit(solution)/shard_map/reduce_scatter | solution.py:262
  105.1 0.5 copy-start.19
  136.3 4.6 copy-start.4
  136.3 4.6 copy-start.20
  136.3 4.6 copy-start.23
  140.9 2.2 copy-start.11
  140.9 2.2 copy-start.12
  140.9 2.0 copy-start.10
  141.0 2.9 copy-start.7
  143.1 0.7 copy-start.2
  145.8 93.8 %reduce-scatter.23.cloned.1.call-start = ((), (), s32[]{:S(2)}) async-start(), calls=%async_computation.21 | async-start | bytes 3981312 | tf_op jit(solution)/shard_map/reduce_scatter | solution.py:264
  147.2 0.7 copy-start.5
  151.2 157.4 %reduce-scatter.19.cloned.1.call-start = ((), (), s32[]{:S(2)}) async-start(), calls=%async_computation.19 | async-start | bytes 7962624 | tf_op jit(solution)/shard_map/reduce_scatter | solution.py:263
  161.0 12.6 %all-to-all-start.2 = ((bf16[1,128,4,192]{1,3,0,2:T(8,128)(2,1)}), bf16[1,128,4,192]{1,3,0,2:T(8,128)(2,1)}, u32[]{:S(2)}, u32[]{:S(2)}) async-start(bf16[1,128,4,192]{1,3,0,2:T(8,128)(2,1)} %bitcast.196), calls=%async_computation.2 | async-start | bytes 393216 | tf_op jit(solution)/shard_map/all_to_all | solution.py:194
  165.6 212.2 %reduce-scatter.11.cloned.1.call-start = ((), (), s32[]{:S(2)}) async-start(), calls=%async_computation.15 | async-start | bytes 7962624 | tf_op jit(solution)/shard_map/reduce_scatter | solution.py:261
  183.9 1.2 copy-start
  197.5 16.4 %copy-start.14 = (f32[128,32]{0,1:T(8,128)S(1)}, f32[128,32]{0,1:T(8,128)}, u32[]{:S(2)}) copy-start(f32[128,32]{0,1:T(8,128)} %get-tuple-element.92) | copy-start | bytes 49156
  197.5 16.4 %copy-start.16 = (f32[128,32]{0,1:T(8,128)S(1)}, f32[128,32]{0,1:T(8,128)}, u32[]{:S(2)}) copy-start(f32[128,32]{0,1:T(8,128)} %get-tuple-element.93) | copy-start | bytes 49156
  198.6 7.8 %collective-permute-start = (bf16[1,1,128,3,1,192]{2,5,0,3,4,1:T(8,128)(2,1)S(1)}, bf16[1,1,128,3,1,192]{2,5,0,3,4,1:T(8,128)(2,1)S(1)}, u32[]{:S(2)}, u32[]{:S(2)}) collective-permute-start(bf16[1,1,128,3,1,192]{2,5,0,3,4,1:T(8,128)(2,1)S(1)} %constant_dynamic-slice_fusion.2), channel_id=1, source_target_pairs={{0,8},{8,16},{16,24},{24,0},{1,9},{9,17},{17,25},{25,1},{2,10},{10... | collective-permute-start | bytes 442376 | tf_op jit(solution)/shard_map/ppermute | solution.py:30
  206.5 7.1 %collective-permute-start.1 = (bf16[1,1,128,3,1,192]{2,5,0,3,4,1:T(8,128)(2,1)S(1)}, bf16[1,1,128,3,1,192]{2,5,0,3,4,1:T(8,128)(2,1)S(1)}, u32[]{:S(2)}, u32[]{:S(2)}) collective-permute-start(bf16[1,1,128,3,1,192]{2,5,0,3,4,1:T(8,128)(2,1)S(1)} %get-tuple-element.78), channel_id=1, source_target_pairs={{0,16},{8,24},{16,0},{24,8},{1,17},{9,25},{17,1},{25,9},{2,18},{10... | collective-permute-start | bytes 442376 | tf_op jit(solution)/shard_map/ppermute | solution.py:30
  206.5 7.0 %collective-permute-start.2 = (bf16[1,1,128,3,1,192]{2,5,0,3,4,1:T(8,128)(2,1)S(1)}, bf16[1,1,128,3,1,192]{2,5,0,3,4,1:T(8,128)(2,1)S(1)}, u32[]{:S(2)}, u32[]{:S(2)}) collective-permute-start(bf16[1,1,128,3,1,192]{2,5,0,3,4,1:T(8,128)(2,1)S(1)} %get-tuple-element.77), channel_id=1, source_target_pairs={{0,24},{8,0},{16,8},{24,16},{1,25},{9,1},{17,9},{25,17},{2,26},{10... | collective-permute-start | bytes 442376 | tf_op jit(solution)/shard_map/ppermute | solution.py:30
  213.6 0.9 copy-start.1
  213.6 0.9 copy-start.18
  213.6 0.9 copy-start.22
  218.7 93.9 %copy-start.6 = (bf16[128,1152]{1,0:T(8,128)(2,1)S(1)}, bf16[128,1152]{1,0:T(8,128)(2,1)}, u32[]{:S(2)}) copy-start(bf16[128,1152]{1,0:T(8,128)(2,1)} %copy-done.5) | copy-start | bytes 884740
  218.7 93.9 %copy-start.9 = (bf16[1152,768]{0,1:T(8,128)(2,1)S(1)}, bf16[1152,768]{0,1:T(8,128)(2,1)}, u32[]{:S(2)}) copy-start(bf16[1152,768]{0,1:T(8,128)(2,1)} %all-gather.11.cloned.1.call-done) | copy-start | bytes 5308420
  218.7 196.4 %reduce-scatter.17.cloned.1.call-start = ((), (), s32[]{:S(2)}) async-start(), calls=%async_computation.18 | async-start | bytes 184320 | tf_op jit(solution)/shard_map/reduce_scatter | solution.py:272
  220.6 209.2 %reduce-scatter.25.cloned.1.call-start = ((), (), s32[]{:S(2)}) async-start(), calls=%async_computation.22 | async-start | bytes 276480
  241.4 204.1 %reduce-scatter.21.cloned.1.call-start = ((), (), s32[]{:S(2)}) async-start(), calls=%async_computation.20 | async-start | bytes 552960 | tf_op jit(solution)/shard_map/reduce_scatter | solution.py:275
  310.7 155.7 %reduce-scatter.13.cloned.1.call-start = ((), (), s32[]{:S(2)}) async-start(), calls=%async_computation.16 | async-start | bytes 552960 | tf_op jit(solution)/shard_map/reduce_scatter | solution.py:269
  314.0 65.8 %copy-start.24 = (f32[768]{0:T(1024)S(1)}, f32[768]{0:T(1024)}, u32[]{:S(2)}) copy-start(f32[768]{0:T(1024)} %get-tuple-element.46) | copy-start | bytes 9220
  314.0 100.3 %copy-start.3 = (f32[128,768]{1,0:T(8,128)S(1)}, f32[128,768]{1,0:T(8,128)}, u32[]{:S(2)}) copy-start(f32[128,768]{1,0:T(8,128)} %copy-done.2) | copy-start | bytes 1179652
Sparse Core Ops, SparseCore 0:
  9.9 36.6 all-gather.4
  48.4 23.9 all-gather.6
  74.3 33.8 all-gather.8
  109.9 26.3 all-gather.10
  145.9 42.3 reduce-scatter.14
  191.6 47.9 reduce-scatter.22
  243.1 65.4 reduce-scatter.18
  312.2 65.4 reduce-scatter.10
  380.0 19.5 reduce-scatter.16
  401.7 17.8 reduce-scatter.24
  422.4 21.0 reduce-scatter.20
  446.3 20.0 reduce-scatter.12
